TPU v7x, 32 devices: a whole 2x2x4 slice. The times are simulated.
32 devices in a mesh: fsdp: 4 (over x, core), tok: 8 (over z, y).
Axes of the slice: x: 2, y: 2, z: 4, core: 2. Of those that a mesh axis runs over, the one named last changes fastest.
Arguments:
- states: bfloat16 [4, 512, 1024], P('fsdp', 'tok'), may hold values from -8 to 8
- cache_keys: bfloat16 [4, 1024, 1024], P('fsdp', 'tok'), may hold values from -6 to 6
- cache_values: bfloat16 [4, 1024, 1024], P('fsdp', 'tok'), may hold values from -6 to 6
- cache_len: int32 [4], P('fsdp'), may hold values from 1 to 1024, as said below
- token_slot: int32 [4, 512], P('fsdp', 'tok'), may hold values from 0 to 511, as said below
- bucket_table: int32 [1536], replicated, may hold values from 0 to 31
- rel_bias: float32 [32, 16], replicated, may hold values from -3 to 250
- norm_gain: float32 [1024], replicated, may hold values from 0.5 to 1.5
- w_query: bfloat16 [1024, 1024], P(('fsdp', 'tok')), may hold values from -0.0234375 to 0.0234375
- w_key: bfloat16 [1024, 1024], P(('fsdp', 'tok')), may hold values from -0.1875 to 0.1875
- w_value: bfloat16 [1024, 1024], P(('fsdp', 'tok')), may hold values from -0.1875 to 0.1875
- w_out: bfloat16 [1024, 1024], P(('fsdp', 'tok')), may hold values from -1.5 to 1.5
Outputs:
- hidden_out: bfloat16 [4, 512, 1024], P('fsdp', 'tok')
- new_keys: bfloat16 [4, 512, 1024], P('fsdp', 'tok')
- new_values: bfloat16 [4, 512, 1024], P('fsdp', 'tok')
Inputs may be any that keep to these rules, and one draw needn't show every extreme that they name: `cache_len`: one request has exactly 1024 live rows. `token_slot`: each row is a permutation of 0 to 511; every aligned block of 64 tokens of a request has exactly 8 of its slots in each aligned block of 64 slots.
All inputs are finite; a program needn't handle non-finite values.
Results may differ from a plain program's by a relative error of at most 0.0095.
Values may be sent and summed in bfloat16 or wider, within the bound.
No kernel may reach another device: no remote copies, remote signals or barrier semaphores. Data moves between devices by JAX's collectives and lax.ppermute only.
A program may use at most 64 MiB of HBM per device.

v0:
```python
import jax
import jax.numpy as jnp
from jax import lax
from jax.sharding import PartitionSpec as P

far_away = 1073741824
neg_floor = -1e30


def bias_scores(bucket_ids, bias_parts):
    bucket_count = bias_parts[0].shape[0]
    one_hot = (bucket_ids[..., None] == jnp.arange(bucket_count, dtype=jnp.int32)).astype(
        jnp.bfloat16
    )
    high_part = jnp.einsum(
        "qkb,bh->hqk", one_hot, bias_parts[0], preferred_element_type=jnp.float32
    )
    middle = jnp.einsum("qkb,bh->hqk", one_hot, bias_parts[1], preferred_element_type=jnp.float32)
    low_part = jnp.einsum("qkb,bh->hqk", one_hot, bias_parts[2], preferred_element_type=jnp.float32)
    return high_part + middle + low_part


def absorb(running, queries, query_pos, keys_here, values_here, key_pos, bucket_table, bias_parts):
    totals, peak_old, masses = running
    head_count = queries.shape[1]
    keys_split = keys_here.reshape(keys_here.shape[0], head_count, -1)
    values_split = values_here.reshape(values_here.shape[0], head_count, -1)
    scores = jnp.einsum("qhd,khd->hqk", queries, keys_split, preferred_element_type=jnp.float32)
    distance = query_pos[:, None] - key_pos[None, :]
    allowed = (distance >= 0)[None]
    bucket_ids = jnp.take(bucket_table, jnp.clip(distance, 0, bucket_table.shape[0] - 1), axis=0)
    scores = scores + bias_scores(bucket_ids, bias_parts)
    new_peak = jnp.maximum(peak_old, jnp.max(jnp.where(allowed, scores, neg_floor), axis=-1))
    weights = jnp.where(allowed, jnp.exp(scores - new_peak[..., None]), 0.0)
    shrink = jnp.exp(peak_old - new_peak)
    masses = masses * shrink + jnp.sum(weights, axis=-1)
    totals = totals * jnp.transpose(shrink)[..., None] + jnp.einsum(
        "hqk,khd->qhd",
        weights.astype(jnp.bfloat16),
        values_split,
        preferred_element_type=jnp.float32,
    )
    return (totals, new_peak, masses)


def permute_rows(selector, rows):
    return jnp.dot(selector.astype(jnp.bfloat16), rows, preferred_element_type=jnp.float32).astype(
        jnp.bfloat16
    )


def permute_ints(selector, values):
    return jnp.sum(jnp.where(selector, values[None, :], 0), axis=1).astype(jnp.int32)


def shards(
    states,
    cache_keys,
    cache_values,
    cache_len,
    token_slot,
    bucket_table,
    rel_bias,
    norm_gain,
    w_query,
    w_key,
    w_value,
    w_out,
):
    peer_count = lax.axis_size("tok")
    my_index = lax.axis_index("tok")
    tokens = states[0]
    tok_rows = tokens.shape[0]
    feature_count = tokens.shape[1]
    per_peer = tok_rows // peer_count
    head_count = rel_bias.shape[1]
    head_size = feature_count // head_count
    slot_ids = token_slot[0]
    length = cache_len[0]
    row_iota = jnp.arange(tok_rows, dtype=jnp.int32)
    ranking = jnp.sum((slot_ids[None, :] < slot_ids[:, None]).astype(jnp.int32), axis=1)
    sort_sel = ranking[None, :] == row_iota[:, None]
    sent_rows = permute_rows(sort_sel, tokens).reshape(peer_count, per_peer, feature_count)
    sent_slots = permute_ints(sort_sel, slot_ids).reshape(peer_count, per_peer)
    sent_pos = (my_index * tok_rows + permute_ints(sort_sel, row_iota)).reshape(
        peer_count, per_peer
    )
    got_rows, got_slots, got_pos = (
        lax.all_to_all(sent_rows, "tok", split_axis=0, concat_axis=0, tiled=True),
        lax.all_to_all(sent_slots, "tok", split_axis=0, concat_axis=0, tiled=True),
        lax.all_to_all(sent_pos, "tok", split_axis=0, concat_axis=0, tiled=True),
    )
    local_slot = got_slots.reshape(tok_rows) - my_index * tok_rows
    place_sel = local_slot[None, :] == row_iota[:, None]
    dealt = permute_rows(place_sel, got_rows.reshape(tok_rows, feature_count))
    dealt_pos = permute_ints(place_sel, got_pos.reshape(tok_rows))
    query_w, key_w, value_w, out_w = (
        lax.all_gather(w_query, ("fsdp", "tok"), axis=0, tiled=True),
        lax.all_gather(w_key, ("fsdp", "tok"), axis=0, tiled=True),
        lax.all_gather(w_value, ("fsdp", "tok"), axis=0, tiled=True),
        lax.all_gather(w_out, ("fsdp", "tok"), axis=0, tiled=True),
    )
    wide_in = dealt.astype(jnp.float32)
    inverse = lax.rsqrt(jnp.mean(wide_in * wide_in, axis=-1, keepdims=True) + 1e-06)
    normed = (wide_in * inverse * norm_gain).astype(jnp.bfloat16)
    queries = jnp.dot(normed, query_w, preferred_element_type=jnp.float32).astype(jnp.bfloat16)
    new_keys = jnp.dot(normed, key_w, preferred_element_type=jnp.float32).astype(jnp.bfloat16)
    new_values = jnp.dot(normed, value_w, preferred_element_type=jnp.float32).astype(jnp.bfloat16)
    query_pos = length + dealt_pos
    cache_rows = cache_keys.shape[1]
    cache_spot = my_index * cache_rows + jnp.arange(cache_rows, dtype=jnp.int32)
    key_pos = jnp.concatenate([jnp.where(cache_spot < length, cache_spot, far_away), query_pos])
    keys_here = jnp.concatenate([cache_keys[0], new_keys])
    values_here = jnp.concatenate([cache_values[0], new_values])
    bias_high = rel_bias.astype(jnp.bfloat16)
    remainder = rel_bias - bias_high.astype(jnp.float32)
    bias_middle = remainder.astype(jnp.bfloat16)
    bias_low = (remainder - bias_middle.astype(jnp.float32)).astype(jnp.bfloat16)
    bias_parts = (bias_high, bias_middle, bias_low)
    query_heads = queries.reshape(tok_rows, head_count, head_size)
    shard_len = keys_here.shape[0]
    initial = (
        jnp.zeros((tok_rows, head_count, head_size), jnp.float32),
        jnp.full((head_count, tok_rows), neg_floor, jnp.float32),
        jnp.zeros((head_count, tok_rows), jnp.float32),
    )
    running = initial
    part_keys = lax.all_gather(keys_here, "tok", axis=0, tiled=True)
    part_values = lax.all_gather(values_here, "tok", axis=0, tiled=True)
    part_pos = lax.all_gather(key_pos, "tok", axis=0, tiled=True)
    rows_in = part_keys.shape[0]
    block_len = 2 * shard_len
    shard_count = rows_in // block_len
    blocks = (
        part_keys.reshape(shard_count, block_len, feature_count),
        part_values.reshape(shard_count, block_len, feature_count),
        part_pos.reshape(shard_count, block_len),
    )

    def advance(running_in, block_set):
        return (
            absorb(
                running_in,
                query_heads,
                query_pos,
                block_set[0],
                block_set[1],
                block_set[2],
                bucket_table,
                bias_parts,
            ),
            None,
        )

    running, unused = lax.scan(advance, running, blocks)
    totals, peaks, masses = running
    context = (
        (totals / jnp.transpose(masses)[..., None])
        .reshape(tok_rows, feature_count)
        .astype(jnp.bfloat16)
    )
    result_dealt = (wide_in + jnp.dot(context, out_w, preferred_element_type=jnp.float32)).astype(
        jnp.bfloat16
    )
    back_rows = permute_rows(jnp.transpose(place_sel), result_dealt).reshape(
        peer_count, per_peer, feature_count
    )
    returned = lax.all_to_all(back_rows, "tok", split_axis=0, concat_axis=0, tiled=True)
    hidden = permute_rows(jnp.transpose(sort_sel), returned.reshape(tok_rows, feature_count))
    return (hidden[None], new_keys[None], new_values[None])


def solution(mesh):
    in_specs = (
        P("fsdp", "tok", None),
        P("fsdp", "tok", None),
        P("fsdp", "tok", None),
        P("fsdp"),
        P("fsdp", "tok"),
        P(),
        P(),
        P(),
        P(("fsdp", "tok"), None),
        P(("fsdp", "tok"), None),
        P(("fsdp", "tok"), None),
        P(("fsdp", "tok"), None),
    )
    out_specs = (P("fsdp", "tok", None), P("fsdp", "tok", None), P("fsdp", "tok", None))
    return jax.shard_map(shards, mesh=mesh, in_specs=in_specs, out_specs=out_specs, check_vma=False)
```

profile of v0, /device:TPU:0, one launch (start us, length us, event | category | flops | bytes accessed | tf_op | source)
XLA Modules:
  0.0 936.9 jit_solution(472488924100509051)
XLA Ops:
  11.8 7.3 all-to-all-start
  19.9 5.6 all-to-all-done
  25.4 3.4 all-to-all-start.1
  29.0 7.2 all-to-all-done.1
  38.0 32.8 %all-gather.13.cloned.1.call-done = bf16[1024,1024]{1,0:T(8,128)(2,1)} async-done(((bf16[32,1024]{1,0:T(8,128)(2,1)}), bf16[1024,1024]{1,0:T(8,128)(2,1)}) %all-gather.13.cloned.1.call-update) | async-done | bytes 2097168 | tf_op jit(solution)/shard_map/all_gather | solution.py:100
  70.8 2.1 convolution_convert_fusion.2
  74.4 54.8 %all-gather.7.cloned.1.call-done = bf16[1024,1024]{1,0:T(8,128)(2,1)} async-done(((bf16[32,1024]{1,0:T(8,128)(2,1)}), bf16[1024,1024]{1,0:T(8,128)(2,1)}) %all-gather.7.cloned.1.call-update) | async-done | bytes 2097168 | tf_op jit(solution)/shard_map/all_gather | solution.py:99
  133.4 4.4 all-to-all-start.2
  140.4 3.7 all-to-all-done.2
  145.7 8.7 all-reduce
  154.4 33.1 %all-gather.11.cloned.1.call-done = bf16[1024,1024]{1,0:T(8,128)(2,1)} async-done(((bf16[32,1024]{1,0:T(8,128)(2,1)}), bf16[1024,1024]{1,0:T(8,128)(2,1)}) %all-gather.11.cloned.1.call-update) | async-done | bytes 2097168 | tf_op jit(solution)/shard_map/all_gather | solution.py:98
  187.6 2.1 convolution_convert_fusion.3
  190.6 58.3 %all-gather.15.cloned.1.call-done = bf16[1536,1024]{1,0:T(8,128)(2,1)} async-done(((bf16[192,1024]{1,0:T(8,128)(2,1)}), bf16[1536,1024]{1,0:T(8,128)(2,1)}) %all-gather.15.cloned.1.call-update) | async-done | bytes 3145744 | tf_op jit(solution)/shard_map/all_gather | solution.py:129
  249.0 61.1 %all-gather.9.cloned.1.call-done = bf16[1536,1024]{1,0:T(8,128)(2,1)} async-done(((bf16[192,1024]{1,0:T(8,128)(2,1)}), bf16[1536,1024]{1,0:T(8,128)(2,1)}) %all-gather.9.cloned.1.call-update) | async-done | bytes 3145744 | tf_op jit(solution)/shard_map/all_gather | solution.py:128
  310.1 605.3 %while.15 = (s32[]{:T(128)}, f32[64,16,64]{0,2,1:T(8,128)}, f32[16,64]{1,0:T(8,128)S(1)}, f32[16,64]{1,0:T(8,128)S(1)}, s32[64]{0:T(128)S(1)}, /*index=5*/s32[4,...) while((s32[]{:T(128)}, f32[64,16,64]{0,2,1:T(8,128)}, ...), condition=%wide.region_8.9_spmd.clone, body=%wide.region_5.8_spmd.clone.sunk | while | flops 183465984 | bytes 27471288 | solution.py:155
  310.3 135.5 %gather_fusion = s32[24576]{0:T(1024)S(1)} fusion(s32[1536]{0:T(1024)S(1)} %get-tuple-element.335, s32[24576]{0:T(1024)S(1)} %broadcast_clamp_fusion.2), kind=kCustom, calls=%fused_computation.clone.clone.1 | custom fusion | bytes 294912 | tf_op jit(solution)/shard_map/while/body/eval_jaxpr/jit(_take)/gather | solution.py:31
  450.1 2.4 constant_dynamic-slice_fusion.3
  453.7 4.1 select_reduce_fusion.5
  460.8 135.5 %gather_fusion = s32[24576]{0:T(1024)S(1)} fusion(s32[1536]{0:T(1024)S(1)} %get-tuple-element.335, s32[24576]{0:T(1024)S(1)} %broadcast_clamp_fusion.2), kind=kCustom, calls=%fused_computation.clone.clone.1 | custom fusion | bytes 294912 | tf_op jit(solution)/shard_map/while/body/eval_jaxpr/jit(_take)/gather | solution.py:31
  600.7 2.4 constant_dynamic-slice_fusion.3
  604.2 4.1 select_reduce_fusion.5
  609.8 2.4 fusion.74
  612.4 135.5 %gather_fusion = s32[24576]{0:T(1024)S(1)} fusion(s32[1536]{0:T(1024)S(1)} %get-tuple-element.335, s32[24576]{0:T(1024)S(1)} %broadcast_clamp_fusion.2), kind=kCustom, calls=%fused_computation.clone.clone.1 | custom fusion | bytes 294912 | tf_op jit(solution)/shard_map/while/body/eval_jaxpr/jit(_take)/gather | solution.py:31
  752.3 2.4 constant_dynamic-slice_fusion.3
  755.8 4.1 select_reduce_fusion.5
  761.4 2.4 fusion.74
  764.0 135.5 %gather_fusion = s32[24576]{0:T(1024)S(1)} fusion(s32[1536]{0:T(1024)S(1)} %get-tuple-element.335, s32[24576]{0:T(1024)S(1)} %broadcast_clamp_fusion.2), kind=kCustom, calls=%fused_computation.clone.clone.1 | custom fusion | bytes 294912 | tf_op jit(solution)/shard_map/while/body/eval_jaxpr/jit(_take)/gather | solution.py:31
  903.9 2.4 constant_dynamic-slice_fusion.3
  907.4 4.1 select_reduce_fusion.5
  913.0 2.4 fusion.74
  916.6 2.2 fusion.25
  918.8 10.4 %all_to_all.25 = bf16[8,8,1024]{2,1,0:T(8,128)(2,1)S(1)} all-to-all(bf16[8,8,1024]{2,1,0:T(8,128)(2,1)S(1)} %fusion.25), channel_id=1, replica_groups=mesh['fsdp'=4,'tok'=8] {'tok'}, dimensions={0} | all-to-all | bytes 262144 | tf_op jit(solution)/shard_map/all_to_all | solution.py:168
  (144 shorter events, 48.4 us)
Async XLA Ops:
  7.2 11.9 %copy-start = (bf16[1,64,1024]{2,1,0:T(8,128)(2,1)S(1)}, bf16[1,64,1024]{2,1,0:T(8,128)(2,1)}, u32[]{:S(2)}) copy-start(bf16[1,64,1024]{2,1,0:T(8,128)(2,1)} %param.14) | copy-start | bytes 393220
  7.2 63.6 %all-gather.13.cloned.1.call-start = ((), (), s32[]{:S(2)}) async-start(), calls=%async_computation.7 | async-start | bytes 2162688 | tf_op jit(solution)/shard_map/all_gather | solution.py:100
  7.9 121.3 %all-gather.7.cloned.1.call-start = ((), (), s32[]{:S(2)}) async-start(), calls=%async_computation.4 | async-start | bytes 2162688 | tf_op jit(solution)/shard_map/all_gather | solution.py:99
  8.7 178.9 %all-gather.11.cloned.1.call-start = ((), (), s32[]{:S(2)}) async-start(), calls=%async_computation.6 | async-start | bytes 2162688 | tf_op jit(solution)/shard_map/all_gather | solution.py:98
  10.3 15.1 %copy-start.11 = (s32[64]{0:T(128)}, s32[64]{0:T(128)S(1)}, u32[]{:S(2)}) copy-start(s32[64]{0:T(128)S(1)} %convert_reduce_fusion) | copy-start | bytes 772
  11.8 13.7 %all-to-all-start = ((s32[8,1,8]{2,1,0:T(1,128)}), s32[8,1,8]{2,1,0:T(1,128)S(1)}, u32[]{:S(2)}, u32[]{:S(2)}) async-start(s32[8,1,8]{2,1,0:T(1,128)} %bitcast.1), calls=%async_computation | async-start | bytes 8192 | tf_op jit(solution)/shard_map/all_to_all | solution.py:90
  25.4 10.8 %all-to-all-start.1 = ((bf16[8,8,1024]{2,1,0:T(8,128)(2,1)}), bf16[8,8,1024]{2,1,0:T(8,128)(2,1)S(1)}, u32[]{:S(2)}, u32[]{:S(2)}) async-start(bf16[8,8,1024]{2,1,0:T(8,128)(2,1)} %fusion.26), calls=%async_computation.1 | async-start | bytes 262144 | tf_op jit(solution)/shard_map/all_to_all | solution.py:89
  28.8 220.1 %all-gather.15.cloned.1.call-start = ((), (), s32[]{:S(2)}) async-start(), calls=%async_computation.8 | async-start | bytes 3538944 | tf_op jit(solution)/shard_map/all_gather | solution.py:129
  29.0 116.4 %copy-start.9 = (s32[64]{0:T(128)}, s32[64]{0:T(128)S(1)}, u32[]{:S(2)}) copy-start(s32[64]{0:T(128)S(1)} %sub.69) | copy-start | bytes 772
  29.0 44.5 %copy-start.6 = (bf16[1,128,1024]{2,1,0:T(8,128)(2,1)S(1)}, bf16[1,128,1024]{2,1,0:T(8,128)(2,1)}, u32[]{:S(2)}) copy-start(bf16[1,128,1024]{2,1,0:T(8,128)(2,1)} %param.16) | copy-start | bytes 786436
  36.5 0.7 copy-start.3
  72.9 0.7 copy-start.4
  74.3 57.6 %copy-start.7 = (bf16[1,128,1024]{2,1,0:T(8,128)(2,1)S(1)}, bf16[1,128,1024]{2,1,0:T(8,128)(2,1)}, u32[]{:S(2)}) copy-start(bf16[1,128,1024]{2,1,0:T(8,128)(2,1)} %param.15) | copy-start | bytes 786436
  74.3 64.7 %copy-start.8 = (f32[32,16]{0,1:T(8,128)S(1)}, f32[32,16]{0,1:T(8,128)}, u32[]{:S(2)}) copy-start(f32[32,16]{0,1:T(8,128)} %param.20) | copy-start | bytes 6148
  74.3 64.7 %copy-start.13 = (u32[32]{0:T(128)S(1)}, u32[32]{0:T(128)}, u32[]{:S(2)}) copy-start(u32[32]{0:T(128)} %constant.64) | copy-start | bytes 388
  74.4 235.7 %all-gather.9.cloned.1.call-start = ((), (), s32[]{:S(2)}) async-start(), calls=%async_computation.5 | async-start | bytes 3538944 | tf_op jit(solution)/shard_map/all_gather | solution.py:128
  131.3 0.7 copy-start.5
  133.4 10.8 %all-to-all-start.2 = ((s32[8,1,8]{2,1,0:T(1,128)}), s32[8,1,8]{2,1,0:T(1,128)S(1)}, u32[]{:S(2)}, u32[]{:S(2)}) async-start(s32[8,1,8]{2,1,0:T(1,128)} %bitcast.6), calls=%async_computation.2 | async-start | bytes 8192 | tf_op jit(solution)/shard_map/all_to_all | solution.py:91
  137.8 778.8 %all-gather.17.cloned.1.call-start = ((), (), s32[]{:S(2)}) async-start(), calls=%async_computation.9 | async-start | bytes 2162688 | tf_op jit(solution)/shard_map/all_gather | solution.py:101
  154.4 155.7 %copy-start.1 = (s32[1536]{0:T(1024)S(1)}, s32[1536]{0:T(1024)}, u32[]{:S(2)}) copy-start(s32[1536]{0:T(1024)} %param.19) | copy-start | bytes 18436
  310.1 606.5 %copy-start.10 = (s32[64]{0:T(128)S(1)}, s32[64]{0:T(128)}, u32[]{:S(2)}) copy-start(s32[64]{0:T(128)} %copy-done.9) | copy-start | bytes 772
  457.8 1.2 copy-start.2
  608.3 1.2 copy-start.2
  759.9 1.2 copy-start.2
  911.5 1.2 copy-start.2
  916.5 12.7 %copy-start.12 = (s32[64]{0:T(128)S(1)}, s32[64]{0:T(128)}, u32[]{:S(2)}) copy-start(s32[64]{0:T(128)} %copy-done.11) | copy-start | bytes 772
Sparse Core Ops, SparseCore 0:
  11.0 59.7 all-gather.12
  73.8 55.3 all-gather.6
  132.2 55.3 all-gather.10
  189.6 59.2 all-gather.14
  251.0 59.0 all-gather.8
  312.9 55.1 all-gather.16
where the time goes:
time: 938 us; the launch traced here: 937 us
  local copies, waits for them, and re-layouts  566 us (60%)
  waiting for transfers between devices  259 us (28%)
  matrix products  51.5 us (5%)
  blocking collectives  19.1 us (2%)
  between operations  15.7 us (2%)
  starting transfers between devices  15.3 us (2%)
  other arithmetic  9.68 us (1%)
    gather x8, local copies, waits for them, and re-layouts, absorb(): jnp.take(bucket_table, jnp.clip(distance, 0, bucket_table.shape[0] - 1),...  542 us
    all_gather x1, waiting for transfers between devices, shards(): part_keys = lax.all_gather(keys_here, 'tok', axis=0, tiled=True)  61.1 us
    all_gather x1, waiting for transfers between devices, shards(): part_values = lax.all_gather(values_here, 'tok', axis=0, tiled=True)  58.3 us
    all_gather x1, waiting for transfers between devices, shards(): lax.all_gather(w_key, ('fsdp', 'tok'), axis=0, tiled=True)  54.8 us
    all_gather x1, waiting for transfers between devices, shards(): lax.all_gather(w_query, ('fsdp', 'tok'), axis=0, tiled=True)  33.1 us
    all_gather x1, waiting for transfers between devices, shards(): lax.all_gather(w_value, ('fsdp', 'tok'), axis=0, tiled=True)  32.8 us
  transfers between devices with their start and end apart: 9, of which 8 were waited for; matrix products, arithmetic and copies ran while one was open for 66% of the time, Pallas kernels for 0%

commit v1 on v0

--- a/solution.py
+++ b/solution.py
@@ -125,7 +125,15 @@
         jnp.zeros((head_count, tok_rows), jnp.float32),
     )
     running = initial
-    part_keys = lax.all_gather(keys_here, "tok", axis=0, tiled=True)
+    k_all = jax.lax.axis_size("tok")
+    chunks = [(nth, (nth + 1) % k_all) for nth in range(k_all)]
+    then = [None] * k_all
+    then[k_all - 1] = keys_here
+    for j0 in range(k_all - 2, -1, -1):
+        then[j0] = jax.lax.ppermute(then[j0 + 1], "tok", chunks)
+    side_arr = jnp.concatenate(then, axis=0)
+    t_next = (jax.lax.axis_index("tok") + 1) * keys_here.shape[0]
+    part_keys = jnp.roll(side_arr, t_next, axis=0)
     part_values = lax.all_gather(values_here, "tok", axis=0, tiled=True)
     part_pos = lax.all_gather(key_pos, "tok", axis=0, tiled=True)
     rows_in = part_keys.shape[0]

time: 938 us -> 899 us (0.958)
  waiting for transfers between devices: 259 us -> 207 us
  local copies, waits for them, and re-layouts: 566 us -> 579 us
    ppermute x0 -> x7, waiting for transfers between devices: none -> 70 us  [shards(): then[j0] = jax.lax.ppermute(then[j0 + 1], 'tok', chunks)]
    all_gather x1 -> x0, waiting for transfers between devices: 61.1 us -> none  [shards(): part_keys = lax.all_gather(keys_here, 'tok', axis=0, tiled=True)]
    all_gather x1, waiting for transfers between devices: 33.1 us -> 0.01 us  [shards(): lax.all_gather(w_query, ('fsdp', 'tok'), axis=0, tiled=True)]
    all_gather x1, waiting for transfers between devices: 58.3 us -> 34.2 us  [shards(): part_values = lax.all_gather(values_here, 'tok', axis=0, tiled=True)]
  transfers between devices with their start and end apart: 9 -> 15, of which waited for: 8 -> 12; matrix products, arithmetic and copies ran while one was open for 66% -> 70% of each run, Pallas kernels for 0% -> 0%
where the time goes in v1:
time: 899 us; the launch traced here: 898 us
  local copies, waits for them, and re-layouts  579 us (64%)
  waiting for transfers between devices  207 us (23%)
  matrix products  45.3 us (5%)
  blocking collectives  22.2 us (2%)
  starting transfers between devices  18.4 us (2%)
  between operations  15.5 us (2%)
  other arithmetic  9.55 us (1%)
    gather x8, local copies, waits for them, and re-layouts, absorb(): jnp.take(bucket_table, jnp.clip(distance, 0, bucket_table.shape[0] - 1),...  542 us
    ppermute x7, waiting for transfers between devices, shards(): then[j0] = jax.lax.ppermute(then[j0 + 1], 'tok', chunks)  70 us
    all_gather x1, waiting for transfers between devices, shards(): lax.all_gather(w_key, ('fsdp', 'tok'), axis=0, tiled=True)  54.8 us
    all_gather x1, waiting for transfers between devices, shards(): part_values = lax.all_gather(values_here, 'tok', axis=0, tiled=True)  34.2 us
    all_gather x1, waiting for transfers between devices, shards(): lax.all_gather(w_value, ('fsdp', 'tok'), axis=0, tiled=True)  32.7 us
    dynamic_slice x16, local copies, waits for them, and re-layouts, shards(): running, unused = lax.scan(advance, running, blocks)  23.4 us
  transfers between devices with their start and end apart: 15, of which 12 were waited for; matrix products, arithmetic and copies ran while one was open for 70% of the time, Pallas kernels for 0%

profile of v1, /device:TPU:0, one launch (start us, length us, event | category | flops | bytes accessed | tf_op | source)
XLA Modules:
  0.0 897.8 jit_solution(18407589133996452013)
XLA Ops:
  11.8 7.3 all-to-all-start
  19.9 5.6 all-to-all-done
  25.5 3.4 all-to-all-start.1
  29.0 7.2 all-to-all-done.1
  38.1 32.7 %all-gather.10.cloned.1.call-done = bf16[1024,1024]{1,0:T(8,128)(2,1)} async-done(((bf16[32,1024]{1,0:T(8,128)(2,1)}), bf16[1024,1024]{1,0:T(8,128)(2,1)}) %all-gather.10.cloned.1.call-update) | async-done | bytes 2097168 | tf_op jit(solution)/shard_map/all_gather | solution.py:100
  74.4 54.8 %all-gather.6.cloned.1.call-done = bf16[1024,1024]{1,0:T(8,128)(2,1)} async-done(((bf16[32,1024]{1,0:T(8,128)(2,1)}), bf16[1024,1024]{1,0:T(8,128)(2,1)}) %all-gather.6.cloned.1.call-update) | async-done | bytes 2097168 | tf_op jit(solution)/shard_map/all_gather | solution.py:99
  132.8 12.8 %collective-permute-done = bf16[192,1024]{1,0:T(8,128)(2,1)S(1)} collective-permute-done((bf16[192,1024]{1,0:T(8,128)(2,1)S(1)}, bf16[192,1024]{1,0:T(8,128)(2,1)S(1)}, u32[]{:S(2)}, u32[]{:S(2)}) %collective-permute-start) | collective-permute-done | bytes 393248 | tf_op jit(solution)/shard_map/ppermute | solution.py:133
  145.6 13.3 %collective-permute-done.1 = bf16[192,1024]{1,0:T(8,128)(2,1)S(1)} collective-permute-done((bf16[192,1024]{1,0:T(8,128)(2,1)S(1)}, bf16[192,1024]{1,0:T(8,128)(2,1)S(1)}, u32[]{:S(2)}, u32[]{:S(2)}) %collective-permute-start.1) | collective-permute-done | bytes 393248 | tf_op jit(solution)/shard_map/ppermute | solution.py:133
  159.0 14.3 %collective-permute-done.2 = bf16[192,1024]{1,0:T(8,128)(2,1)S(1)} collective-permute-done((bf16[192,1024]{1,0:T(8,128)(2,1)S(1)}, bf16[192,1024]{1,0:T(8,128)(2,1)S(1)}, u32[]{:S(2)}, u32[]{:S(2)}) %collective-permute-start.2) | collective-permute-done | bytes 393248 | tf_op jit(solution)/shard_map/ppermute | solution.py:133
  173.3 10.5 %collective-permute-done.3 = bf16[192,1024]{1,0:T(8,128)(2,1)S(1)} collective-permute-done((bf16[192,1024]{1,0:T(8,128)(2,1)S(1)}, bf16[192,1024]{1,0:T(8,128)(2,1)S(1)}, u32[]{:S(2)}, u32[]{:S(2)}) %collective-permute-start.3) | collective-permute-done | bytes 393248 | tf_op jit(solution)/shard_map/ppermute | solution.py:133
  184.5 6.0 all-to-all-start.2
  192.3 7.6 collective-permute-done.4
  202.6 10.1 %collective-permute-done.5 = bf16[192,1024]{1,0:T(8,128)(2,1)S(1)} collective-permute-done((bf16[192,1024]{1,0:T(8,128)(2,1)S(1)}, bf16[192,1024]{1,0:T(8,128)(2,1)S(1)}, u32[]{:S(2)}, u32[]{:S(2)}) %collective-permute-start.5) | collective-permute-done | bytes 393248 | tf_op jit(solution)/shard_map/ppermute | solution.py:133
  212.8 11.8 %all-reduce = s32[1536]{0:T(1024)S(1)} all-reduce(s32[1536]{0:T(1024)S(1)} %add_dynamic-update-slice_fusion), channel_id=1, replica_groups=mesh['fsdp'=4,'tok'=8] {'tok'}, use_global_device_ids=true, to_apply=%add | all-reduce | flops 1536 | bytes 12288
  225.2 2.1 convolution_convert_fusion.3
  232.0 2.6 constant_dynamic-slice_fusion.2
  234.6 34.2 %all-gather.12.cloned.1.call-done = bf16[1536,1024]{1,0:T(8,128)(2,1)} async-done(((bf16[192,1024]{1,0:T(8,128)(2,1)}), bf16[1536,1024]{1,0:T(8,128)(2,1)}) %all-gather.12.cloned.1.call-update) | async-done | bytes 3145744 | tf_op jit(solution)/shard_map/all_gather | solution.py:137
  268.8 607.9 %while.15 = (s32[]{:T(128)}, f32[64,16,64]{0,2,1:T(8,128)}, f32[16,64]{1,0:T(8,128)S(1)}, f32[16,64]{1,0:T(8,128)S(1)}, s32[64]{0:T(128)S(1)}, /*index=5*/s32[4,...) while((s32[]{:T(128)}, f32[64,16,64]{0,2,1:T(8,128)}, ...), condition=%wide.region_8.9_spmd.clone, body=%wide.region_5.8_spmd.clone.sunk | while | flops 183465984 | bytes 26422740 | solution.py:163
  269.6 135.5 %gather_fusion = s32[24576]{0:T(1024)S(1)} fusion(s32[1536]{0:T(1024)S(1)} %get-tuple-element.335, s32[24576]{0:T(1024)S(1)} %broadcast_clamp_fusion.2), kind=kCustom, calls=%fused_computation.clone.clone.1 | custom fusion | bytes 294912 | tf_op jit(solution)/shard_map/while/body/eval_jaxpr/jit(_take)/gather | solution.py:31
  409.5 2.4 constant_dynamic-slice_fusion.4
  413.1 4.1 select_reduce_fusion.5
  421.6 135.5 %gather_fusion = s32[24576]{0:T(1024)S(1)} fusion(s32[1536]{0:T(1024)S(1)} %get-tuple-element.335, s32[24576]{0:T(1024)S(1)} %broadcast_clamp_fusion.2), kind=kCustom, calls=%fused_computation.clone.clone.1 | custom fusion | bytes 294912 | tf_op jit(solution)/shard_map/while/body/eval_jaxpr/jit(_take)/gather | solution.py:31
  561.5 2.4 constant_dynamic-slice_fusion.4
  565.1 4.1 select_reduce_fusion.5
  573.6 135.5 %gather_fusion = s32[24576]{0:T(1024)S(1)} fusion(s32[1536]{0:T(1024)S(1)} %get-tuple-element.335, s32[24576]{0:T(1024)S(1)} %broadcast_clamp_fusion.2), kind=kCustom, calls=%fused_computation.clone.clone.1 | custom fusion | bytes 294912 | tf_op jit(solution)/shard_map/while/body/eval_jaxpr/jit(_take)/gather | solution.py:31
  713.4 2.4 constant_dynamic-slice_fusion.4
  717.1 4.1 select_reduce_fusion.5
  725.5 135.5 %gather_fusion = s32[24576]{0:T(1024)S(1)} fusion(s32[1536]{0:T(1024)S(1)} %get-tuple-element.335, s32[24576]{0:T(1024)S(1)} %broadcast_clamp_fusion.2), kind=kCustom, calls=%fused_computation.clone.clone.1 | custom fusion | bytes 294912 | tf_op jit(solution)/shard_map/while/body/eval_jaxpr/jit(_take)/gather | solution.py:31
  865.4 2.4 constant_dynamic-slice_fusion.4
  869.0 4.1 select_reduce_fusion.5
  877.8 2.2 fusion.25
  880.0 10.4 %all_to_all.25 = bf16[8,8,1024]{2,1,0:T(8,128)(2,1)S(1)} all-to-all(bf16[8,8,1024]{2,1,0:T(8,128)(2,1)S(1)} %fusion.25), channel_id=1, replica_groups=mesh['fsdp'=4,'tok'=8] {'tok'}, dimensions={0} | all-to-all | bytes 262144 | tf_op jit(solution)/shard_map/all_to_all | solution.py:176
  (192 shorter events, 64.7 us)
Async XLA Ops:
  7.2 11.9 %copy-start = (bf16[1,64,1024]{2,1,0:T(8,128)(2,1)S(1)}, bf16[1,64,1024]{2,1,0:T(8,128)(2,1)}, u32[]{:S(2)}) copy-start(bf16[1,64,1024]{2,1,0:T(8,128)(2,1)} %param.14) | copy-start | bytes 393220
  7.2 66.4 %copy-start.8 = (bf16[1,128,1024]{2,1,0:T(8,128)(2,1)S(1)}, bf16[1,128,1024]{2,1,0:T(8,128)(2,1)}, u32[]{:S(2)}) copy-start(bf16[1,128,1024]{2,1,0:T(8,128)(2,1)} %param.16) | copy-start | bytes 786436
  7.2 63.6 %all-gather.10.cloned.1.call-start = ((), (), s32[]{:S(2)}) async-start(), calls=%async_computation.6 | async-start | bytes 2162688 | tf_op jit(solution)/shard_map/all_gather | solution.py:100
  7.9 121.3 %all-gather.6.cloned.1.call-start = ((), (), s32[]{:S(2)}) async-start(), calls=%async_computation.4 | async-start | bytes 2162688 | tf_op jit(solution)/shard_map/all_gather | solution.py:99
  8.7 216.6 %all-gather.8.cloned.1.call-start = ((), (), s32[]{:S(2)}) async-start(), calls=%async_computation.5 | async-start | bytes 2162688 | tf_op jit(solution)/shard_map/all_gather | solution.py:98
  10.3 15.1 %copy-start.17 = (s32[64]{0:T(128)}, s32[64]{0:T(128)S(1)}, u32[]{:S(2)}) copy-start(s32[64]{0:T(128)S(1)} %convert_reduce_fusion) | copy-start | bytes 772
  11.8 13.7 %all-to-all-start = ((s32[8,1,8]{2,1,0:T(1,128)}), s32[8,1,8]{2,1,0:T(1,128)S(1)}, u32[]{:S(2)}, u32[]{:S(2)}) async-start(s32[8,1,8]{2,1,0:T(1,128)} %bitcast.1), calls=%async_computation | async-start | bytes 8192 | tf_op jit(solution)/shard_map/all_to_all | solution.py:90
  25.5 10.8 %all-to-all-start.1 = ((bf16[8,8,1024]{2,1,0:T(8,128)(2,1)}), bf16[8,8,1024]{2,1,0:T(8,128)(2,1)S(1)}, u32[]{:S(2)}, u32[]{:S(2)}) async-start(bf16[8,8,1024]{2,1,0:T(8,128)(2,1)} %fusion.26), calls=%async_computation.1 | async-start | bytes 262144 | tf_op jit(solution)/shard_map/all_to_all | solution.py:89
  28.8 239.9 %all-gather.12.cloned.1.call-start = ((), (), s32[]{:S(2)}) async-start(), calls=%async_computation.7 | async-start | bytes 3538944 | tf_op jit(solution)/shard_map/all_gather | solution.py:137
  29.0 173.5 %copy-start.15 = (s32[64]{0:T(128)}, s32[64]{0:T(128)S(1)}, u32[]{:S(2)}) copy-start(s32[64]{0:T(128)S(1)} %sub.73) | copy-start | bytes 772
  37.2 94.1 %copy-start.4 = (bf16[1,128,1024]{2,1,0:T(8,128)(2,1)S(1)}, bf16[1,128,1024]{2,1,0:T(8,128)(2,1)}, u32[]{:S(2)}) copy-start(bf16[1,128,1024]{2,1,0:T(8,128)(2,1)} %param.15) | copy-start | bytes 786436
  38.0 153.7 %copy-start.14 = (f32[32,16]{0,1:T(8,128)S(1)}, f32[32,16]{0,1:T(8,128)}, u32[]{:S(2)}) copy-start(f32[32,16]{0,1:T(8,128)} %param.20) | copy-start | bytes 6148
  38.0 161.9 %copy-start.19 = (u32[32]{0:T(128)S(1)}, u32[32]{0:T(128)}, u32[]{:S(2)}) copy-start(u32[32]{0:T(128)} %constant.86) | copy-start | bytes 388
  131.3 100.6 %copy-start.6 = (bf16[64,1024]{1,0:T(8,128)(2,1)}, bf16[64,1024]{1,0:T(8,128)(2,1)S(1)}, u32[]{:S(2)}) copy-start(bf16[64,1024]{1,0:T(8,128)(2,1)S(1)} %convolution_convert_fusion.4) | copy-start | bytes 393220
  131.3 14.3 %collective-permute-start = (bf16[192,1024]{1,0:T(8,128)(2,1)S(1)}, bf16[192,1024]{1,0:T(8,128)(2,1)S(1)}, u32[]{:S(2)}, u32[]{:S(2)}) collective-permute-start(bf16[192,1024]{1,0:T(8,128)(2,1)S(1)} %pad_maximum_fusion), channel_id=1, source_target_pairs={{0,1},{1,2},{2,3},{3,4},{4,5},{5,6},{6,7},{7,0},{8,9},{9,10},{10,1... | collective-permute-start | bytes 1179656 | tf_op jit(solution)/shard_map/ppermute | solution.py:133
  145.6 13.3 %collective-permute-start.1 = (bf16[192,1024]{1,0:T(8,128)(2,1)S(1)}, bf16[192,1024]{1,0:T(8,128)(2,1)S(1)}, u32[]{:S(2)}, u32[]{:S(2)}) collective-permute-start(bf16[192,1024]{1,0:T(8,128)(2,1)S(1)} %collective-permute-done), channel_id=1, source_target_pairs={{0,1},{1,2},{2,3},{3,4},{4,5},{5,6},{6,7},{7,0},{8,9},{9,10},{10,1... | collective-permute-start | bytes 1179656 | tf_op jit(solution)/shard_map/ppermute | solution.py:133
  159.0 14.3 %collective-permute-start.2 = (bf16[192,1024]{1,0:T(8,128)(2,1)S(1)}, bf16[192,1024]{1,0:T(8,128)(2,1)S(1)}, u32[]{:S(2)}, u32[]{:S(2)}) collective-permute-start(bf16[192,1024]{1,0:T(8,128)(2,1)S(1)} %collective-permute-done.1), channel_id=1, source_target_pairs={{0,1},{1,2},{2,3},{3,4},{4,5},{5,6},{6,7},{7,0},{8,9},{9,10},{10,1... | collective-permute-start | bytes 1179656 | tf_op jit(solution)/shard_map/ppermute | solution.py:133
  173.3 10.5 %collective-permute-start.3 = (bf16[192,1024]{1,0:T(8,128)(2,1)S(1)}, bf16[192,1024]{1,0:T(8,128)(2,1)S(1)}, u32[]{:S(2)}, u32[]{:S(2)}) collective-permute-start(bf16[192,1024]{1,0:T(8,128)(2,1)S(1)} %collective-permute-done.2), channel_id=1, source_target_pairs={{0,1},{1,2},{2,3},{3,4},{4,5},{5,6},{6,7},{7,0},{8,9},{9,10},{10,1... | collective-permute-start | bytes 1179656 | tf_op jit(solution)/shard_map/ppermute | solution.py:133
  183.8 16.1 %collective-permute-start.4 = (bf16[192,1024]{1,0:T(8,128)(2,1)S(1)}, bf16[192,1024]{1,0:T(8,128)(2,1)S(1)}, u32[]{:S(2)}, u32[]{:S(2)}) collective-permute-start(bf16[192,1024]{1,0:T(8,128)(2,1)S(1)} %collective-permute-done.3), channel_id=1, source_target_pairs={{0,1},{1,2},{2,3},{3,4},{4,5},{5,6},{6,7},{7,0},{8,9},{9,10},{10,1... | collective-permute-start | bytes 1179656 | tf_op jit(solution)/shard_map/ppermute | solution.py:133
  184.5 16.7 %all-to-all-start.2 = ((s32[8,1,8]{2,1,0:T(1,128)}), s32[8,1,8]{2,1,0:T(1,128)S(1)}, u32[]{:S(2)}, u32[]{:S(2)}) async-start(s32[8,1,8]{2,1,0:T(1,128)} %bitcast.6), calls=%async_computation.2 | async-start | bytes 8192 | tf_op jit(solution)/shard_map/all_to_all | solution.py:91
  190.5 687.3 %all-gather.14.cloned.1.call-start = ((), (), s32[]{:S(2)}) async-start(), calls=%async_computation.8 | async-start | bytes 2162688 | tf_op jit(solution)/shard_map/all_gather | solution.py:101
  199.9 12.8 %collective-permute-start.5 = (bf16[192,1024]{1,0:T(8,128)(2,1)S(1)}, bf16[192,1024]{1,0:T(8,128)(2,1)S(1)}, u32[]{:S(2)}, u32[]{:S(2)}) collective-permute-start(bf16[192,1024]{1,0:T(8,128)(2,1)S(1)} %collective-permute-done.4), channel_id=1, source_target_pairs={{0,1},{1,2},{2,3},{3,4},{4,5},{5,6},{6,7},{7,0},{8,9},{9,10},{10,1... | collective-permute-start | bytes 1179656 | tf_op jit(solution)/shard_map/ppermute | solution.py:133
  202.6 22.6 %copy-start.12 = (s32[64]{0:T(128)}, s32[64]{0:T(128)S(1)}, u32[]{:S(2)}) copy-start(s32[64]{0:T(128)S(1)} %broadcast_add_fusion.1) | copy-start | bytes 772
  212.7 18.6 %collective-permute-start.6 = (bf16[192,1024]{1,0:T(8,128)(2,1)S(1)}, bf16[192,1024]{1,0:T(8,128)(2,1)S(1)}, u32[]{:S(2)}, u32[]{:S(2)}) collective-permute-start(bf16[192,1024]{1,0:T(8,128)(2,1)S(1)} %collective-permute-done.5), channel_id=1, source_target_pairs={{0,1},{1,2},{2,3},{3,4},{4,5},{5,6},{6,7},{7,0},{8,9},{9,10},{10,1... | collective-permute-start | bytes 1179656 | tf_op jit(solution)/shard_map/ppermute | solution.py:133
  231.9 36.8 %copy-start.1 = (s32[1536]{0:T(1024)S(1)}, s32[1536]{0:T(1024)}, u32[]{:S(2)}) copy-start(s32[1536]{0:T(1024)} %param.19) | copy-start | bytes 18436
  231.9 36.8 %copy-start.9 = (bf16[32,16]{0,1:T(8,128)(2,1)S(1)}, bf16[32,16]{0,1:T(8,128)(2,1)}, u32[]{:S(2)}) copy-start(bf16[32,16]{0,1:T(8,128)(2,1)} %get-tuple-element.308) | copy-start | bytes 3076
  231.9 36.8 %copy-start.10 = (bf16[32,16]{0,1:T(8,128)(2,1)S(1)}, bf16[32,16]{0,1:T(8,128)(2,1)}, u32[]{:S(2)}) copy-start(bf16[32,16]{0,1:T(8,128)(2,1)} %get-tuple-element.307) | copy-start | bytes 3076
  232.0 36.8 %copy-start.11 = (bf16[32,16]{0,1:T(8,128)(2,1)S(1)}, bf16[32,16]{0,1:T(8,128)(2,1)}, u32[]{:S(2)}) copy-start(bf16[32,16]{0,1:T(8,128)(2,1)} %get-tuple-element.306) | copy-start | bytes 3076
  232.0 36.8 %copy-start.13 = (s32[64]{0:T(128)S(1)}, s32[64]{0:T(128)}, u32[]{:S(2)}) copy-start(s32[64]{0:T(128)} %copy-done.12) | copy-start | bytes 772
  268.8 609.0 %copy-start.16 = (s32[64]{0:T(128)S(1)}, s32[64]{0:T(128)}, u32[]{:S(2)}) copy-start(s32[64]{0:T(128)} %copy-done.15) | copy-start | bytes 772
  417.2 2.1 copy-start.2
  876.6 13.8 %copy-start.18 = (s32[64]{0:T(128)S(1)}, s32[64]{0:T(128)}, u32[]{:S(2)}) copy-start(s32[64]{0:T(128)} %copy-done.17) | copy-start | bytes 772
  (9 other events, 11.0 us)
Sparse Core Ops, SparseCore 0:
  11.0 59.7 all-gather.9
  73.8 55.3 all-gather.5
  132.2 68.8 all-gather.7
  203.1 65.6 all-gather.11
  271.5 55.1 all-gather.13
